TPU v7x, 128 devices: a whole 4x4x4 slice. The times are simulated.
128 devices in a mesh: row: 16 (over z_lo, y, core), col: 8 (over x, z_hi).
Axes of the slice: x: 4, y: 4, z: 4 (z_hi: 2, z_lo: 2; z = z_hi * 2 + z_lo), core: 2. Of those that a mesh axis runs over, the one named last changes fastest.
Arguments:
- features: bfloat16 [32768, 128], P(('col', 'row')), may hold values from -6 to 6
- weight: bfloat16 [128, 256], replicated, may hold values from -0.5 to 0.5
- adj_values: bfloat16 [12288, 256, 256], P(('row', 'col')), may hold values from -0.0390625 to 0.0390625
- slot_rows: int32 [12288], P(('row', 'col')), may hold values from 0 to 7, as said below
- slot_cols: int32 [12288], P(('row', 'col')), may hold values from 0 to 15
- slot_live: int32 [128], P(('row', 'col')), may hold values from 13 to 96, as said below
- cotangent: bfloat16 [32768, 256], P(('row', 'col')), may hold values from -6 to 6
Outputs:
- output: bfloat16 [32768, 256], P(('row', 'col'))
- grad_features: bfloat16 [32768, 128], P(('col', 'row'))
- grad_weight: float32 [128, 256], replicated
Inputs may be any that keep to these rules, and one draw needn't show every extreme that they name: Within one device's slots the pairs (slot_rows, slot_cols) are distinct. `slot_live`: some device has all 96 slots live.
All inputs are finite; a program needn't handle non-finite values.
Results may differ from a plain program's by a relative error of at most 0.006.
Values may be sent and summed in bfloat16 or wider, within the bound.
A program may use at most 128 MiB of HBM per device.

v0:
```python
import math
import jax
import jax.numpy as jnp
from jax import lax
from jax.sharding import PartitionSpec as P


def silu_slope(value):
    sig = jax.nn.sigmoid(value)
    return sig * (1.0 + value * (1.0 - sig))


def block_product(adj_values, index_in, index_out, keep, source, count_out, transposed):
    slots, size = (adj_values.shape[0], adj_values.shape[1])
    width = source.shape[2]
    group = math.gcd(slots, 32)
    groups = slots // group

    def step(total, item):
        values, taken, placed, weights = item
        picked = source[taken]
        if transposed:
            product = jnp.einsum("sab,saf->sbf", values, picked, preferred_element_type=jnp.float32)
        else:
            product = jnp.einsum("sab,sbf->saf", values, picked, preferred_element_type=jnp.float32)
        return (total.at[placed].add(product * weights[:, None, None]), None)

    items = (
        adj_values.reshape(groups, group, size, size),
        index_in.reshape(groups, group),
        index_out.reshape(groups, group),
        keep.reshape(groups, group),
    )
    total, _ = lax.scan(step, jnp.zeros((count_out, size, width), jnp.float32), items)
    return total.reshape(count_out * size, width)


def body(features, weight, adj_values, slot_rows, slot_cols, slot_live, cotangent):
    size = adj_values.shape[1]
    slots = adj_values.shape[0]
    width = weight.shape[1]
    own_rows = features.shape[0]
    per_device = own_rows // size
    tile_rows = per_device * lax.axis_size("col")
    tile_cols = per_device * lax.axis_size("row")
    nodes = own_rows * lax.axis_size("row") * lax.axis_size("col")
    keep = (jnp.arange(slots, dtype=jnp.int32) < slot_live[0]).astype(jnp.float32)
    projected = jnp.dot(features, weight, preferred_element_type=jnp.float32).astype(jnp.bfloat16)
    column_rows = lax.all_gather(projected, "row", axis=0, tiled=True)
    column_blocks = column_rows.reshape(tile_cols, size, width)
    partial_value = block_product(
        adj_values, slot_cols, slot_rows, keep, column_blocks, tile_rows, False
    )
    summed = lax.psum_scatter(partial_value, "col", scatter_dimension=0, tiled=True)
    output = jax.nn.silu(summed).astype(jnp.bfloat16)
    grad_summed = (cotangent.astype(jnp.float32) * silu_slope(summed)).astype(jnp.bfloat16)
    grad_range = lax.all_gather(grad_summed, "col", axis=0, tiled=True)
    grad_blocks = grad_range.reshape(tile_rows, size, width)
    back = block_product(adj_values, slot_rows, slot_cols, keep, grad_blocks, tile_cols, True)
    grad_projected = lax.psum_scatter(back, "row", scatter_dimension=0, tiled=True).astype(
        jnp.bfloat16
    )
    grad_features = jnp.dot(grad_projected, weight.T, preferred_element_type=jnp.float32).astype(
        jnp.bfloat16
    )
    local_term = lax.dot_general(
        features, grad_projected, (((0,), (0,)), ((), ())), preferred_element_type=jnp.float32
    )
    grad_weight = lax.psum(local_term, ("row", "col")) / math.sqrt(nodes)
    return (output, grad_features, grad_weight)


def solution(mesh):
    placed = (
        P(("col", "row"), None),
        P(),
        P(("row", "col"), None, None),
        P(("row", "col")),
        P(("row", "col")),
        P(("row", "col")),
        P(("row", "col"), None),
    )
    return jax.shard_map(
        body,
        mesh=mesh,
        in_specs=placed,
        out_specs=(P(("row", "col"), None), P(("col", "row"), None), P()),
        check_vma=False,
    )
```

profile of v0, /device:TPU:1, one launch (start us, length us, event | category | flops | bytes accessed | tf_op | source)
XLA Modules:
  0.0 557.0 jit_solution(4911130216952027264)
XLA Ops:
  7.2 0.0 copy-start
  7.2 0.0 all-gather.3.cloned.1.call-start
  7.2 0.8 copy-done
  8.0 1.7 convolution_convert_fusion
  9.7 0.0 all-gather.3.cloned.1.call-update
  9.7 0.0 reduce-scatter.3.cloned.1.call-start
  10.4 0.7 reshape.149
  11.1 0.7 reshape.151
  11.9 35.7 %all-gather.3.cloned.1.call-done = bf16[4096,256]{1,0:T(8,128)(2,1)} async-done(((bf16[256,256]{1,0:T(8,128)(2,1)}), bf16[4096,256]{1,0:T(8,128)(2,1)}) %all-gather.3.cloned.1.call-update) | async-done | bytes 2097168 | tf_op jit(solution)/shard_map/all_gather | solution.py:49
  47.6 0.2 broadcast_in_dim.4
  47.8 0.0 copy-start.4
  47.8 72.4 %while.20 = (s32[]{:T(128)}, f32[8,256,256]{2,1,0:T(8,128)S(1)}, s32[3,32]{1,0:T(4,128)S(1)}, bf16[3,32,256,256]{3,2,1,0:T(8,128)(2,1)}, s32[3,32]{1,0:T(4,128)S...) while((s32[]{:T(128)}, f32[8,256,256]{2,1,0:T(8,128)S(1)}, s32[3,32]{1,0:T(4,128)S(1)}, ...), condition=%wide.region_2.3_spmd, body=%wide.region_0.2_spmd.sunk | while | flops 1077937408 | bytes 50337628 | solution.py:34
  47.8 4.4 gather_fusion
  52.2 7.9 %broadcast_multiply_fusion.5 = f32[32,256,256]{2,1,0:T(8,128)} fusion(f32[32]{0:T(128)S(1)} %fusion.42, bf16[32,256,256]{2,1,0:T(8,128)(2,1)} %gather_fusion, bf16[3,32,256,256]{3,2,1,0:T(8,128)(2,1)} %get-tuple-element.236, s32[]{:T(128)} %get-tuple-element.225), kind=kOutput, calls=%fused_computation.6.clone.1 | convolution fusion | flops 1075838976 | bytes 16777856 | tf_op jit(solution)/shard_map/while/body/eval_jaxpr/sab,sbf->saf/dot_general | solution.py:25
  60.2 11.8 %scatter_fusion = f32[8,256,256]{2,1,0:T(8,128)S(1)} fusion(f32[8,256,256]{2,1,0:T(8,128)S(1)} %get-tuple-element.226, s32[32]{0:T(128)S(1)} %get-tuple-element.206, f32[32,256,256]{2,1,0:T(8,128)} %broadcast_multiply_fusion.5), kind=kCustom, calls=%fused_computation.2.clone.1 | custom fusion | flops 2097152 | bytes 25165952 | tf_op jit(solution)/shard_map/while/body/eval_jaxpr/scatter-add | solution.py:26
  72.0 4.4 gather_fusion
  76.4 7.9 %broadcast_multiply_fusion.5 = f32[32,256,256]{2,1,0:T(8,128)} fusion(f32[32]{0:T(128)S(1)} %fusion.42, bf16[32,256,256]{2,1,0:T(8,128)(2,1)} %gather_fusion, bf16[3,32,256,256]{3,2,1,0:T(8,128)(2,1)} %get-tuple-element.236, s32[]{:T(128)} %get-tuple-element.225), kind=kOutput, calls=%fused_computation.6.clone.1 | convolution fusion | flops 1075838976 | bytes 16777856 | tf_op jit(solution)/shard_map/while/body/eval_jaxpr/sab,sbf->saf/dot_general | solution.py:25
  84.3 11.7 %scatter_fusion = f32[8,256,256]{2,1,0:T(8,128)S(1)} fusion(f32[8,256,256]{2,1,0:T(8,128)S(1)} %get-tuple-element.226, s32[32]{0:T(128)S(1)} %get-tuple-element.206, f32[32,256,256]{2,1,0:T(8,128)} %broadcast_multiply_fusion.5), kind=kCustom, calls=%fused_computation.2.clone.1 | custom fusion | flops 2097152 | bytes 25165952 | tf_op jit(solution)/shard_map/while/body/eval_jaxpr/scatter-add | solution.py:26
  96.1 4.4 gather_fusion
  100.5 7.9 %broadcast_multiply_fusion.5 = f32[32,256,256]{2,1,0:T(8,128)} fusion(f32[32]{0:T(128)S(1)} %fusion.42, bf16[32,256,256]{2,1,0:T(8,128)(2,1)} %gather_fusion, bf16[3,32,256,256]{3,2,1,0:T(8,128)(2,1)} %get-tuple-element.236, s32[]{:T(128)} %get-tuple-element.225), kind=kOutput, calls=%fused_computation.6.clone.1 | convolution fusion | flops 1075838976 | bytes 16777856 | tf_op jit(solution)/shard_map/while/body/eval_jaxpr/sab,sbf->saf/dot_general | solution.py:25
  108.4 11.7 %scatter_fusion = f32[8,256,256]{2,1,0:T(8,128)S(1)} fusion(f32[8,256,256]{2,1,0:T(8,128)S(1)} %get-tuple-element.226, s32[32]{0:T(128)S(1)} %get-tuple-element.206, f32[32,256,256]{2,1,0:T(8,128)} %broadcast_multiply_fusion.5), kind=kCustom, calls=%fused_computation.2.clone.1 | custom fusion | flops 2097152 | bytes 25165952 | tf_op jit(solution)/shard_map/while/body/eval_jaxpr/scatter-add | solution.py:26
  120.2 0.0 copy-start.1
  120.2 1.3 copy-done.1
  121.5 0.0 reduce-scatter.3.cloned.1.call-update
  121.6 0.0 all-gather.5.cloned.1.call-start
  121.6 75.0 %reduce-scatter.3.cloned.1.call-done = f32[256,256]{1,0:T(8,128)} async-done(((f32[2048,256]{1,0:T(8,128)}), f32[256,256]{1,0:T(8,128)}) %reduce-scatter.3.cloned.1.call-update) | async-done | bytes 262160 | tf_op jit(solution)/shard_map/reduce_scatter | solution.py:54
  196.6 0.0 copy-done.4
  196.6 1.8 multiply_convert_fusion
  198.4 0.0 all-gather.5.cloned.1.call-update
  198.4 0.0 reduce-scatter.5.cloned.1.call-start
  198.5 16.6 %copy.10 = bf16[96,256,256]{1,2,0:T(8,128)(2,1)} copy(bf16[96,256,256]{2,1,0:T(8,128)(2,1)} %bitcast.87) | data formatting | bytes 25165824 | tf_op args[2]
  215.1 30.2 %all-gather.5.cloned.1.call-done = bf16[2048,256]{1,0:T(8,128)(2,1)} async-done(((bf16[256,256]{1,0:T(8,128)(2,1)}), bf16[2048,256]{1,0:T(8,128)(2,1)}) %all-gather.5.cloned.1.call-update) | async-done | bytes 1048592 | tf_op jit(solution)/shard_map/all_gather | solution.py:57
  245.3 0.0 copy-start.2
  245.3 2.4 broadcast_in_dim.8
  247.7 0.0 copy-done.2
  247.7 87.2 %while.21 = (s32[]{:T(128)}, f32[16,256,256]{2,1,0:T(8,128)}, s32[3,32]{1,0:T(4,128)S(1)}, bf16[3,32,256,256]{2,3,1,0:T(8,128)(2,1)}, s32[3,32]{1,0:T(4,128)S(1)...) while((s32[]{:T(128)}, f32[16,256,256]{2,1,0:T(8,128)}, s32[3,32]{1,0:T(4,128)S(1)}, ...), condition=%wide.region_6.7_spmd, body=%wide.region_4.6_spmd.sunk | while | flops 1077937408 | bytes 50337628 | solution.py:34
  247.7 2.8 gather_fusion.1
  250.5 7.9 %broadcast_multiply_fusion.6 = f32[32,256,256]{2,1,0:T(8,128)} fusion(f32[32]{0:T(128)S(1)} %fusion.46, bf16[32,256,256]{2,1,0:T(8,128)(2,1)} %gather_fusion.1, bf16[3,32,256,256]{2,3,1,0:T(8,128)(2,1)} %get-tuple-element.260, s32[]{:T(128)} %get-tuple-element.249), kind=kOutput, calls=%fused_computation.22.clone.1 | convolution fusion | flops 1075838976 | bytes 16777856 | tf_op jit(solution)/shard_map/while/body/eval_jaxpr/sab,saf->sbf/dot_general | solution.py:23
  258.4 18.5 %scatter_fusion.1 = f32[16,256,256]{2,1,0:T(8,128)} fusion(f32[16,256,256]{2,1,0:T(8,128)} %get-tuple-element.250, s32[32]{0:T(128)S(1)} %get-tuple-element.215, f32[32,256,256]{2,1,0:T(8,128)} %broadcast_multiply_fusion.6), kind=kCustom, calls=%fused_computation.3.clone.1 | custom fusion | flops 2097152 | bytes 25165952 | tf_op jit(solution)/shard_map/while/body/eval_jaxpr/scatter-add | solution.py:26
  277.0 2.8 gather_fusion.1
  279.8 7.9 %broadcast_multiply_fusion.6 = f32[32,256,256]{2,1,0:T(8,128)} fusion(f32[32]{0:T(128)S(1)} %fusion.46, bf16[32,256,256]{2,1,0:T(8,128)(2,1)} %gather_fusion.1, bf16[3,32,256,256]{2,3,1,0:T(8,128)(2,1)} %get-tuple-element.260, s32[]{:T(128)} %get-tuple-element.249), kind=kOutput, calls=%fused_computation.22.clone.1 | convolution fusion | flops 1075838976 | bytes 16777856 | tf_op jit(solution)/shard_map/while/body/eval_jaxpr/sab,saf->sbf/dot_general | solution.py:23
  287.7 18.3 %scatter_fusion.1 = f32[16,256,256]{2,1,0:T(8,128)} fusion(f32[16,256,256]{2,1,0:T(8,128)} %get-tuple-element.250, s32[32]{0:T(128)S(1)} %get-tuple-element.215, f32[32,256,256]{2,1,0:T(8,128)} %broadcast_multiply_fusion.6), kind=kCustom, calls=%fused_computation.3.clone.1 | custom fusion | flops 2097152 | bytes 25165952 | tf_op jit(solution)/shard_map/while/body/eval_jaxpr/scatter-add | solution.py:26
  306.0 2.8 gather_fusion.1
  308.8 7.9 %broadcast_multiply_fusion.6 = f32[32,256,256]{2,1,0:T(8,128)} fusion(f32[32]{0:T(128)S(1)} %fusion.46, bf16[32,256,256]{2,1,0:T(8,128)(2,1)} %gather_fusion.1, bf16[3,32,256,256]{2,3,1,0:T(8,128)(2,1)} %get-tuple-element.260, s32[]{:T(128)} %get-tuple-element.249), kind=kOutput, calls=%fused_computation.22.clone.1 | convolution fusion | flops 1075838976 | bytes 16777856 | tf_op jit(solution)/shard_map/while/body/eval_jaxpr/sab,saf->sbf/dot_general | solution.py:23
  316.7 18.2 %scatter_fusion.1 = f32[16,256,256]{2,1,0:T(8,128)} fusion(f32[16,256,256]{2,1,0:T(8,128)} %get-tuple-element.250, s32[32]{0:T(128)S(1)} %get-tuple-element.215, f32[32,256,256]{2,1,0:T(8,128)} %broadcast_multiply_fusion.6), kind=kCustom, calls=%fused_computation.3.clone.1 | custom fusion | flops 2097152 | bytes 25165952 | tf_op jit(solution)/shard_map/while/body/eval_jaxpr/scatter-add | solution.py:26
  334.9 0.0 copy-start.3
  334.9 0.0 reduce-scatter.5.cloned.1.call-update
  335.0 0.0 all-reduce.2.cloned.1.call-start
  335.0 64.2 %reduce-scatter.5.cloned.1.call-done = f32[256,256]{1,0:T(8,128)} async-done(((f32[4096,256]{1,0:T(8,128)}), f32[256,256]{1,0:T(8,128)}) %reduce-scatter.5.cloned.1.call-update) | async-done | bytes 262160 | tf_op jit(solution)/shard_map/reduce_scatter | solution.py:60
  399.2 1.8 convolution_bitcast_fusion
  401.1 0.0 all-reduce.2.cloned.1.call-update
  401.1 0.0 copy-done.3
  401.1 1.8 convolution_convert_fusion.1
  402.9 145.9 %all-reduce.2.cloned.1.call-done = f32[128,256]{0,1:T(8,128)} async-done(((f32[128,256]{0,1:T(8,128)}), f32[128,256]{0,1:T(8,128)}) %all-reduce.2.cloned.1.call-update) | async-done | bytes 131088 | tf_op jit(solution)/shard_map/psum | solution.py:69
  548.8 0.9 broadcast_multiply_fusion.2
  549.7 0.8 copy.12
  (19 shorter events, 0.1 us)
Async XLA Ops:
  7.2 0.8 copy-start
  7.2 40.4 %all-gather.3.cloned.1.call-start = ((), (), s32[]{:S(2)}) async-start(), calls=%async_computation.2 | async-start | bytes 2228224 | tf_op jit(solution)/shard_map/all_gather | solution.py:49
  9.7 186.9 %reduce-scatter.3.cloned.1.call-start = ((), (), s32[]{:S(2)}) async-start(), calls=%async_computation.3 | async-start | bytes 2359296 | tf_op jit(solution)/shard_map/reduce_scatter | solution.py:54
  47.8 148.9 %copy-start.4 = (bf16[256,256]{1,0:T(8,128)(2,1)S(1)}, bf16[256,256]{1,0:T(8,128)(2,1)}, u32[]{:S(2)}) copy-start(bf16[256,256]{1,0:T(8,128)(2,1)} %param.17) | copy-start | bytes 393220
  120.2 1.3 copy-start.1
  121.6 123.7 %all-gather.5.cloned.1.call-start = ((), (), s32[]{:S(2)}) async-start(), calls=%async_computation.4 | async-start | bytes 1179648 | tf_op jit(solution)/shard_map/all_gather | solution.py:57
  198.4 200.8 %reduce-scatter.5.cloned.1.call-start = ((), (), s32[]{:S(2)}) async-start(), calls=%async_computation.5 | async-start | bytes 4456448 | tf_op jit(solution)/shard_map/reduce_scatter | solution.py:60
  245.3 2.4 copy-start.2
  334.9 66.1 %copy-start.3 = (bf16[128,256]{1,0:T(8,128)(2,1)S(1)}, bf16[128,256]{1,0:T(8,128)(2,1)}, u32[]{:S(2)}) copy-start(bf16[128,256]{1,0:T(8,128)(2,1)} %param.12) | copy-start | bytes 196612
  335.0 213.8 %all-reduce.2.cloned.1.call-start = ((), (), s32[]{:S(2)}) async-start(), calls=%async_computation.6 | async-start | bytes 262144 | tf_op jit(solution)/shard_map/psum | solution.py:69
Sparse Core Ops, SparseCore 0:
  10.3 37.2 all-gather.2
  121.7 74.9 reduce-scatter.2
  199.6 45.6 all-gather.4
  335.1 64.0 reduce-scatter.4
  404.4 144.3 all-reduce.1
where the time goes:
time: 558 us; the launch traced here: 557 us
  waiting for transfers between devices  351 us (63%)
  other arithmetic  93.1 us (17%)
  matrix products  52.9 us (9%)
  local copies, waits for them, and re-layouts  45.1 us (8%)
  between operations  14.5 us (3%)
    psum x1, waiting for transfers between devices, body(): grad_weight = lax.psum(local_term, ('row', 'col')) / math.sqrt(nodes)  146 us
    scatter-add x6, other arithmetic, step(): return (total.at[placed].add(product * weights[:, None, None]), None)  90.3 us
    reduce_scatter x1, waiting for transfers between devices, body(): lax.psum_scatter(partial_value, 'col', scatter_dimension=0, tiled=True)  75 us
    reduce_scatter x1, waiting for transfers between devices, body(): lax.psum_scatter(back, 'row', scatter_dimension=0, tiled=True)  64.2 us
    all_gather x1, waiting for transfers between devices, body(): column_rows = lax.all_gather(projected, 'row', axis=0, tiled=True)  35.7 us
    all_gather x1, waiting for transfers between devices, body(): grad_range = lax.all_gather(grad_summed, 'col', axis=0, tiled=True)  30.2 us
    dot_general x3, matrix products, step(): jnp.einsum('sab,sbf->saf', values, picked, preferred_element_type=jnp.flo...  23.8 us
    dot_general x3, matrix products, step(): jnp.einsum('sab,saf->sbf', values, picked, preferred_element_type=jnp.flo...  23.8 us
  transfers between devices with their start and end apart: 5, of which 5 were waited for; matrix products, arithmetic and copies ran while one was open for 4% of the time, Pallas kernels for 0%

commit v1 on v0

--- a/solution.py
+++ b/solution.py
@@ -66,7 +66,9 @@
     local_term = lax.dot_general(
         features, grad_projected, (((0,), (0,)), ((), ())), preferred_element_type=jnp.float32
     )
-    grad_weight = lax.psum(local_term, ("row", "col")) / math.sqrt(nodes)
+    grad_weight = jax.lax.all_gather(local_term, axis_name=("row", "col")).sum(axis=0) / math.sqrt(
+        nodes
+    )
     return (output, grad_features, grad_weight)
 
 

time: 558 us -> 739 us (1.32)
  waiting for transfers between devices: 351 us -> 511 us
  local copies, waits for them, and re-layouts: 45.1 us -> 59.2 us
  other arithmetic: 93.1 us -> 101 us
    all_gather x0 -> x1, waiting for transfers between devices: none -> 305 us  [body(): jax.lax.all_gather(local_term, axis_name=('row', 'col')).sum(axis=0)]
    psum x1 -> x0, waiting for transfers between devices: 146 us -> none  [body(): grad_weight = lax.psum(local_term, ('row', 'col')) / math.sqrt(nodes)]
    unnamed x12 -> x13, local copies, waits for them, and re-layouts: 19.5 us -> 33.6 us
    reduce_sum x0 -> x1, other arithmetic: none -> 8.39 us  [body(): jax.lax.all_gather(local_term, axis_name=('row', 'col')).sum(axis=0)]
  transfers between devices with their start and end apart: 5 -> 5, of which waited for: 5 -> 5; matrix products, arithmetic and copies ran while one was open for 4% -> 3% of each run, Pallas kernels for 0% -> 0%
where the time goes in v1:
time: 739 us; the launch traced here: 738 us
  waiting for transfers between devices  511 us (69%)
  other arithmetic  101 us (14%)
  local copies, waits for them, and re-layouts  59.2 us (8%)
  matrix products  52.9 us (7%)
  between operations  14.5 us (2%)
    all_gather x1, waiting for transfers between devices, body(): jax.lax.all_gather(local_term, axis_name=('row', 'col')).sum(axis=0)  305 us
    scatter-add x6, other arithmetic, step(): return (total.at[placed].add(product * weights[:, None, None]), None)  90.3 us
    reduce_scatter x1, waiting for transfers between devices, body(): lax.psum_scatter(partial_value, 'col', scatter_dimension=0, tiled=True)  75.1 us
    reduce_scatter x1, waiting for transfers between devices, body(): lax.psum_scatter(back, 'row', scatter_dimension=0, tiled=True)  64.2 us
    all_gather x1, waiting for transfers between devices, body(): column_rows = lax.all_gather(projected, 'row', axis=0, tiled=True)  35.7 us
    unnamed x13, local copies, waits for them, and re-layouts  33.6 us
    all_gather x1, waiting for transfers between devices, body(): grad_range = lax.all_gather(grad_summed, 'col', axis=0, tiled=True)  30.1 us
    dot_general x3, matrix products, step(): jnp.einsum('sab,sbf->saf', values, picked, preferred_element_type=jnp.flo...  23.8 us
  transfers between devices with their start and end apart: 5, of which 5 were waited for; matrix products, arithmetic and copies ran while one was open for 3% of the time, Pallas kernels for 0%

profile of v1, /device:TPU:1, one launch (start us, length us, event | category | flops | bytes accessed | tf_op | source)
XLA Modules:
  0.0 738.0 jit_solution(4248810342634226336)
XLA Ops:
  7.2 0.0 copy-start
  7.2 0.0 all-gather.5.cloned.1.call-start
  7.2 0.8 copy-done
  8.0 1.7 convolution_convert_fusion
  9.7 0.0 all-gather.5.cloned.1.call-update
  9.7 0.0 reduce-scatter.3.cloned.1.call-start
  10.4 0.7 reshape.149
  11.1 0.7 reshape.151
  11.9 35.7 %all-gather.5.cloned.1.call-done = bf16[4096,256]{1,0:T(8,128)(2,1)} async-done(((bf16[256,256]{1,0:T(8,128)(2,1)}), bf16[4096,256]{1,0:T(8,128)(2,1)}) %all-gather.5.cloned.1.call-update) | async-done | bytes 2097168 | tf_op jit(solution)/shard_map/all_gather | solution.py:49
  47.6 0.2 broadcast_in_dim.4
  47.8 0.0 copy-start.4
  47.8 72.4 %while.20 = (s32[]{:T(128)}, f32[8,256,256]{2,1,0:T(8,128)S(1)}, s32[3,32]{1,0:T(4,128)S(1)}, bf16[3,32,256,256]{3,2,1,0:T(8,128)(2,1)}, s32[3,32]{1,0:T(4,128)S...) while((s32[]{:T(128)}, f32[8,256,256]{2,1,0:T(8,128)S(1)}, s32[3,32]{1,0:T(4,128)S(1)}, ...), condition=%wide.region_2.3_spmd, body=%wide.region_0.2_spmd.sunk | while | flops 1077937408 | bytes 50337128 | solution.py:34
  47.8 4.4 gather_fusion
  52.2 7.9 %broadcast_multiply_fusion.5 = f32[32,256,256]{2,1,0:T(8,128)} fusion(f32[32]{0:T(128)S(1)} %fusion.42, bf16[32,256,256]{2,1,0:T(8,128)(2,1)} %gather_fusion, bf16[3,32,256,256]{3,2,1,0:T(8,128)(2,1)} %get-tuple-element.243, s32[]{:T(128)S(6)} %copy.21), kind=kOutput, calls=%fused_computation.6.clone.1 | convolution fusion | flops 1075838976 | bytes 16777348 | tf_op jit(solution)/shard_map/while/body/eval_jaxpr/sab,sbf->saf/dot_general | solution.py:25
  60.2 11.8 %scatter_fusion = f32[8,256,256]{2,1,0:T(8,128)S(1)} fusion(f32[8,256,256]{2,1,0:T(8,128)S(1)} %get-tuple-element.233, s32[32]{0:T(128)S(1)} %get-tuple-element.213, f32[32,256,256]{2,1,0:T(8,128)} %broadcast_multiply_fusion.5), kind=kCustom, calls=%fused_computation.2.clone.1 | custom fusion | flops 2097152 | bytes 25165952 | tf_op jit(solution)/shard_map/while/body/eval_jaxpr/scatter-add | solution.py:26
  72.0 4.4 gather_fusion
  76.4 7.9 %broadcast_multiply_fusion.5 = f32[32,256,256]{2,1,0:T(8,128)} fusion(f32[32]{0:T(128)S(1)} %fusion.42, bf16[32,256,256]{2,1,0:T(8,128)(2,1)} %gather_fusion, bf16[3,32,256,256]{3,2,1,0:T(8,128)(2,1)} %get-tuple-element.243, s32[]{:T(128)S(6)} %copy.21), kind=kOutput, calls=%fused_computation.6.clone.1 | convolution fusion | flops 1075838976 | bytes 16777348 | tf_op jit(solution)/shard_map/while/body/eval_jaxpr/sab,sbf->saf/dot_general | solution.py:25
  84.3 11.7 %scatter_fusion = f32[8,256,256]{2,1,0:T(8,128)S(1)} fusion(f32[8,256,256]{2,1,0:T(8,128)S(1)} %get-tuple-element.233, s32[32]{0:T(128)S(1)} %get-tuple-element.213, f32[32,256,256]{2,1,0:T(8,128)} %broadcast_multiply_fusion.5), kind=kCustom, calls=%fused_computation.2.clone.1 | custom fusion | flops 2097152 | bytes 25165952 | tf_op jit(solution)/shard_map/while/body/eval_jaxpr/scatter-add | solution.py:26
  96.1 4.4 gather_fusion
  100.5 7.9 %broadcast_multiply_fusion.5 = f32[32,256,256]{2,1,0:T(8,128)} fusion(f32[32]{0:T(128)S(1)} %fusion.42, bf16[32,256,256]{2,1,0:T(8,128)(2,1)} %gather_fusion, bf16[3,32,256,256]{3,2,1,0:T(8,128)(2,1)} %get-tuple-element.243, s32[]{:T(128)S(6)} %copy.21), kind=kOutput, calls=%fused_computation.6.clone.1 | convolution fusion | flops 1075838976 | bytes 16777348 | tf_op jit(solution)/shard_map/while/body/eval_jaxpr/sab,sbf->saf/dot_general | solution.py:25
  108.5 11.7 %scatter_fusion = f32[8,256,256]{2,1,0:T(8,128)S(1)} fusion(f32[8,256,256]{2,1,0:T(8,128)S(1)} %get-tuple-element.233, s32[32]{0:T(128)S(1)} %get-tuple-element.213, f32[32,256,256]{2,1,0:T(8,128)} %broadcast_multiply_fusion.5), kind=kCustom, calls=%fused_computation.2.clone.1 | custom fusion | flops 2097152 | bytes 25165952 | tf_op jit(solution)/shard_map/while/body/eval_jaxpr/scatter-add | solution.py:26
  120.2 0.0 copy-start.1
  120.2 1.3 copy-done.1
  121.6 0.0 reduce-scatter.3.cloned.1.call-update
  121.6 0.0 all-gather.7.cloned.1.call-start
  121.6 75.1 %reduce-scatter.3.cloned.1.call-done = f32[256,256]{1,0:T(8,128)} async-done(((f32[2048,256]{1,0:T(8,128)}), f32[256,256]{1,0:T(8,128)}) %reduce-scatter.3.cloned.1.call-update) | async-done | bytes 262160 | tf_op jit(solution)/shard_map/reduce_scatter | solution.py:54
  196.7 0.0 copy-done.4
  196.7 1.8 multiply_convert_fusion
  198.5 0.0 all-gather.7.cloned.1.call-update
  198.5 0.0 reduce-scatter.5.cloned.1.call-start
  198.6 16.6 %copy.12 = bf16[96,256,256]{1,2,0:T(8,128)(2,1)} copy(bf16[96,256,256]{2,1,0:T(8,128)(2,1)} %bitcast.92) | data formatting | bytes 25165824 | tf_op args[2]
  215.2 30.1 %all-gather.7.cloned.1.call-done = bf16[2048,256]{1,0:T(8,128)(2,1)} async-done(((bf16[256,256]{1,0:T(8,128)(2,1)}), bf16[2048,256]{1,0:T(8,128)(2,1)}) %all-gather.7.cloned.1.call-update) | async-done | bytes 1048592 | tf_op jit(solution)/shard_map/all_gather | solution.py:57
  245.3 0.0 copy-start.2
  245.3 2.4 broadcast_in_dim.8
  247.7 0.0 copy-done.2
  247.7 87.3 %while.21 = (s32[]{:T(128)}, f32[16,256,256]{2,1,0:T(8,128)}, s32[3,32]{1,0:T(4,128)S(1)}, bf16[3,32,256,256]{2,3,1,0:T(8,128)(2,1)}, s32[3,32]{1,0:T(4,128)S(1)...) while((s32[]{:T(128)}, f32[16,256,256]{2,1,0:T(8,128)}, s32[3,32]{1,0:T(4,128)S(1)}, ...), condition=%wide.region_6.7_spmd, body=%wide.region_4.6_spmd.sunk | while | flops 1077937408 | bytes 50337128 | solution.py:34
  247.8 2.8 gather_fusion.1
  250.5 7.9 %broadcast_multiply_fusion.6 = f32[32,256,256]{2,1,0:T(8,128)} fusion(f32[32]{0:T(128)S(1)} %fusion.46, bf16[32,256,256]{2,1,0:T(8,128)(2,1)} %gather_fusion.1, bf16[3,32,256,256]{2,3,1,0:T(8,128)(2,1)} %get-tuple-element.267, s32[]{:T(128)S(6)} %copy.27), kind=kOutput, calls=%fused_computation.22.clone.1 | convolution fusion | flops 1075838976 | bytes 16777348 | tf_op jit(solution)/shard_map/while/body/eval_jaxpr/sab,saf->sbf/dot_general | solution.py:23
  258.5 18.5 %scatter_fusion.1 = f32[16,256,256]{2,1,0:T(8,128)} fusion(f32[16,256,256]{2,1,0:T(8,128)} %get-tuple-element.257, s32[32]{0:T(128)S(1)} %get-tuple-element.222, f32[32,256,256]{2,1,0:T(8,128)} %broadcast_multiply_fusion.6), kind=kCustom, calls=%fused_computation.3.clone.1 | custom fusion | flops 2097152 | bytes 25165952 | tf_op jit(solution)/shard_map/while/body/eval_jaxpr/scatter-add | solution.py:26
  277.0 2.8 gather_fusion.1
  279.8 7.9 %broadcast_multiply_fusion.6 = f32[32,256,256]{2,1,0:T(8,128)} fusion(f32[32]{0:T(128)S(1)} %fusion.46, bf16[32,256,256]{2,1,0:T(8,128)(2,1)} %gather_fusion.1, bf16[3,32,256,256]{2,3,1,0:T(8,128)(2,1)} %get-tuple-element.267, s32[]{:T(128)S(6)} %copy.27), kind=kOutput, calls=%fused_computation.22.clone.1 | convolution fusion | flops 1075838976 | bytes 16777348 | tf_op jit(solution)/shard_map/while/body/eval_jaxpr/sab,saf->sbf/dot_general | solution.py:23
  287.7 18.3 %scatter_fusion.1 = f32[16,256,256]{2,1,0:T(8,128)} fusion(f32[16,256,256]{2,1,0:T(8,128)} %get-tuple-element.257, s32[32]{0:T(128)S(1)} %get-tuple-element.222, f32[32,256,256]{2,1,0:T(8,128)} %broadcast_multiply_fusion.6), kind=kCustom, calls=%fused_computation.3.clone.1 | custom fusion | flops 2097152 | bytes 25165952 | tf_op jit(solution)/shard_map/while/body/eval_jaxpr/scatter-add | solution.py:26
  306.1 2.8 gather_fusion.1
  308.8 7.9 %broadcast_multiply_fusion.6 = f32[32,256,256]{2,1,0:T(8,128)} fusion(f32[32]{0:T(128)S(1)} %fusion.46, bf16[32,256,256]{2,1,0:T(8,128)(2,1)} %gather_fusion.1, bf16[3,32,256,256]{2,3,1,0:T(8,128)(2,1)} %get-tuple-element.267, s32[]{:T(128)S(6)} %copy.27), kind=kOutput, calls=%fused_computation.22.clone.1 | convolution fusion | flops 1075838976 | bytes 16777348 | tf_op jit(solution)/shard_map/while/body/eval_jaxpr/sab,saf->sbf/dot_general | solution.py:23
  316.8 18.2 %scatter_fusion.1 = f32[16,256,256]{2,1,0:T(8,128)} fusion(f32[16,256,256]{2,1,0:T(8,128)} %get-tuple-element.257, s32[32]{0:T(128)S(1)} %get-tuple-element.222, f32[32,256,256]{2,1,0:T(8,128)} %broadcast_multiply_fusion.6), kind=kCustom, calls=%fused_computation.3.clone.1 | custom fusion | flops 2097152 | bytes 25165952 | tf_op jit(solution)/shard_map/while/body/eval_jaxpr/scatter-add | solution.py:26
  335.0 0.0 copy-start.3
  335.0 0.0 reduce-scatter.5.cloned.1.call-update
  335.0 0.0 all-gather.9.cloned.1.call-start
  335.1 64.2 %reduce-scatter.5.cloned.1.call-done = f32[256,256]{1,0:T(8,128)} async-done(((f32[4096,256]{1,0:T(8,128)}), f32[256,256]{1,0:T(8,128)}) %reduce-scatter.5.cloned.1.call-update) | async-done | bytes 262160 | tf_op jit(solution)/shard_map/reduce_scatter | solution.py:60
  399.3 1.8 convolution_bitcast_fusion
  401.1 0.0 all-gather.9.cloned.1.call-update
  401.1 0.0 copy-done.3
  401.1 1.8 convolution_convert_fusion.1
  402.9 305.3 %all-gather.9.cloned.1.call-done = f32[16384,256]{0,1:T(8,128)} async-done(((f32[128,256]{0,1:T(8,128)}), f32[16384,256]{0,1:T(8,128)}) %all-gather.9.cloned.1.call-update) | async-done | bytes 16777232 | tf_op jit(solution)/shard_map/all_gather | solution.py:69
  708.2 14.1 %copy.16 = f32[32,8,128,128]{3,2,1,0:T(8,128)} copy(f32[32,8,128,128]{3,1,2,0:T(8,128)} %bitcast.94) | data formatting | bytes 33554432
  722.3 8.4 %bitcast_reduce_fusion = f32[128,256]{0,1:T(8,128)S(1)} fusion(f32[32,8,128,128]{3,2,1,0:T(8,128)} %copy.16), kind=kLoop, calls=%fused_computation.36 | loop fusion | flops 4161536 | bytes 16908288 | tf_op jit(solution)/shard_map/reduce_sum | solution.py:69
  730.7 0.8 copy.14
  (20 shorter events, 0.2 us)
Async XLA Ops:
  7.2 0.8 copy-start
  7.2 40.4 %all-gather.5.cloned.1.call-start = ((), (), s32[]{:S(2)}) async-start(), calls=%async_computation.2 | async-start | bytes 2228224 | tf_op jit(solution)/shard_map/all_gather | solution.py:49
  9.7 187.0 %reduce-scatter.3.cloned.1.call-start = ((), (), s32[]{:S(2)}) async-start(), calls=%async_computation.3 | async-start | bytes 2359296 | tf_op jit(solution)/shard_map/reduce_scatter | solution.py:54
  47.8 149.0 %copy-start.4 = (bf16[256,256]{1,0:T(8,128)(2,1)S(1)}, bf16[256,256]{1,0:T(8,128)(2,1)}, u32[]{:S(2)}) copy-start(bf16[256,256]{1,0:T(8,128)(2,1)} %param.17) | copy-start | bytes 393220
  120.2 1.3 copy-start.1
  121.6 123.7 %all-gather.7.cloned.1.call-start = ((), (), s32[]{:S(2)}) async-start(), calls=%async_computation.4 | async-start | bytes 1179648 | tf_op jit(solution)/shard_map/all_gather | solution.py:57
  198.5 200.7 %reduce-scatter.5.cloned.1.call-start = ((), (), s32[]{:S(2)}) async-start(), calls=%async_computation.5 | async-start | bytes 4456448 | tf_op jit(solution)/shard_map/reduce_scatter | solution.py:60
  245.3 2.4 copy-start.2
  335.0 66.1 %copy-start.3 = (bf16[128,256]{1,0:T(8,128)(2,1)S(1)}, bf16[128,256]{1,0:T(8,128)(2,1)}, u32[]{:S(2)}) copy-start(bf16[128,256]{1,0:T(8,128)(2,1)} %param.12) | copy-start | bytes 196612
  335.0 373.2 %all-gather.9.cloned.1.call-start = ((), (), s32[]{:S(2)}) async-start(), calls=%async_computation.6 | async-start | bytes 16908288 | tf_op jit(solution)/shard_map/all_gather | solution.py:69
Sparse Core Ops, SparseCore 0:
  10.3 37.2 all-gather.4
  121.7 74.9 reduce-scatter.2
  199.6 45.6 all-gather.6
  335.1 64.0 reduce-scatter.4
  401.3 306.8 all-gather.8
